TPU v7x, 256 devices: a whole 4x4x8 slice. The times are simulated.
256 devices in a mesh: dp: 8 (over z_lo, core), seq: 16 (over x, y), mp: 2 (over z_hi).
Axes of the slice: x: 4, y: 4, z: 8 (z_hi: 2, z_lo: 4; z = z_hi * 4 + z_lo), core: 2. Of those that a mesh axis runs over, the one named last changes fastest.
Arguments:
- features: bfloat16 [8, 8192, 1408], P('dp', ('seq', 'mp')), may hold values from -6 to 6
- conv_weight: bfloat16 [5, 1408, 1536], P(None, ('seq', 'mp')), may hold values from -0.0625 to 0.0625
- norm_gain: float32 [1536], replicated, may hold values from 0.25 to 1.75
- query_weight: bfloat16 [1536, 1024], replicated, may hold values from -0.15625 to 0.15625
- keyval_weight: bfloat16 [1536, 320], replicated, may hold values from -0.15625 to 0.15625
- head_scale: float32 [8], replicated, may hold values from 0.5 to 24
- output_weight: bfloat16 [1536, 1536], replicated, may hold values from -0.15625 to 0.15625
- pair_weight: bfloat16 [1536, 256], replicated, may hold values from -0.625 to 0.625
- pair_input: bfloat16 [8, 256, 256, 128], P('dp', ('seq', 'mp')), may hold values from -6 to 6
- flip_weight: bfloat16 [128, 128], replicated, may hold values from -0.5 to 0.5
- pair_cotangent: bfloat16 [8, 256, 256, 128], P('dp', ('seq', 'mp')), may hold values from -0.0234375 to 0.0234375
Outputs:
- block_out: bfloat16 [8, 4096, 1536], P('dp', ('seq', 'mp'))
- pair_out: bfloat16 [8, 256, 256, 128], P('dp', ('seq', 'mp'))
- grad_flip: float32 [128, 128], replicated
All inputs are finite; a program needn't handle non-finite values.
Results may differ from a plain program's by a relative error of at most 0.011.
Values may be sent and summed in bfloat16 or wider, within the bound.
A program may use at most 192 MiB of HBM per device.

v0:
```python
import math
import jax
import jax.numpy as jnp
from jax import lax
from jax.sharding import PartitionSpec as P

PAIR_POOL = 16
norm_eps = 1e-06
logit_cap = 50.0


def padded_2(shard, sides, width):
    for axis, dim in sides:
        devices, length = (lax.axis_size(axis), shard.shape[dim])
        up = [(i, (i + 1) % devices) for i in range(devices - 1)]
        down = [(j, i) for i, j in up]
        last = lax.slice_in_dim(shard, length - width, length, axis=dim)
        initial = lax.slice_in_dim(shard, 0, width, axis=dim)
        before = lax.ppermute(last, axis, up)
        after = lax.ppermute(initial, axis, down)
        shard = jnp.concatenate([before, shard, after], axis=dim)
    return shard


def root_norm(values_in):
    return values_in * lax.rsqrt(jnp.mean(values_in * values_in, axis=-1, keepdims=True) + norm_eps)


def prepare(raw):
    return jax.nn.gelu(root_norm(raw.astype(jnp.float32)), approximate=False).astype(jnp.bfloat16)


def tap_sum(source, out_rows, tap_count, running, filter_rows):
    for lag_index in range(tap_count):
        running = running + jnp.dot(
            source[lag_index : lag_index + out_rows],
            filter_rows[lag_index],
            preferred_element_type=jnp.float32,
        )
    return running


def per_device(
    features,
    conv_weight,
    norm_gain,
    query_weight,
    keyval_weight,
    head_scale,
    output_weight,
    pair_weight,
    pair_input,
    flip_weight,
    pair_cotangent,
):
    fine_rows = features.shape[1]
    coarse_rows = fine_rows // 2
    in_channels = features.shape[2]
    model_dim = output_weight.shape[1]
    head_count = head_scale.shape[0]
    key_dim = query_weight.shape[1] // head_count
    pair_dim = flip_weight.shape[0]
    tap_count = conv_weight.shape[0]
    margin = tap_count // 2
    padded = padded_2(features, ((("seq", "mp"), 1),), margin)
    prepared = prepare(padded[0])
    starting = jnp.zeros((fine_rows, model_dim), jnp.float32)
    conv_sum = tap_sum(
        prepared,
        fine_rows,
        tap_count,
        starting,
        lax.all_gather(conv_weight, ("seq", "mp"), axis=1, tiled=True),
    )
    skipped = jnp.pad(features[0].astype(jnp.float32), ((0, 0), (0, model_dim - in_channels)))
    encoded = jnp.max((conv_sum + skipped).reshape(coarse_rows, 2, model_dim), axis=1).astype(
        jnp.bfloat16
    )
    widened = encoded.astype(jnp.float32)
    normed = (root_norm(widened) * norm_gain).astype(jnp.bfloat16)
    scale_row = jnp.repeat(head_scale, key_dim) / math.sqrt(key_dim)
    queries = (
        jnp.dot(normed, query_weight, preferred_element_type=jnp.float32) * scale_row
    ).astype(jnp.bfloat16)
    keyvals = jnp.dot(normed, keyval_weight, preferred_element_type=jnp.float32).astype(
        jnp.bfloat16
    )
    pooled = jnp.mean(
        widened.reshape(coarse_rows // PAIR_POOL, PAIR_POOL, model_dim), axis=1
    ).astype(jnp.bfloat16)
    pair_feats = jnp.dot(pooled, pair_weight, preferred_element_type=jnp.float32).astype(
        jnp.bfloat16
    )
    pair_q = pair_feats[:, :pair_dim]
    pair_k = pair_feats[:, pair_dim:]
    keys_all, pairk_all = (
        lax.all_gather(keyvals[None], ("seq", "mp"), axis=1, tiled=True),
        lax.all_gather(pair_k[None], ("seq", "mp"), axis=1, tiled=True),
    )
    summed = (
        pair_input[0].astype(jnp.float32)
        + pair_q[:, None, :].astype(jnp.float32) * pairk_all[0][None, :, :].astype(jnp.float32)
    ).astype(jnp.bfloat16)
    flipped = lax.all_to_all(summed[None], ("seq", "mp"), split_axis=2, concat_axis=1, tiled=True)[
        0
    ]
    turned = jnp.einsum("bac,cd->abd", flipped, flip_weight, preferred_element_type=jnp.float32)
    pair_out = (summed.astype(jnp.float32) + turned).astype(jnp.bfloat16)
    grad_term = jnp.einsum(
        "bac,abd->cd", flipped, pair_cotangent[0], preferred_element_type=jnp.float32
    )
    grad_flip = lax.psum(grad_term, ("dp", "seq", "mp"))
    key_rows = keys_all[0][:, :key_dim]
    value_rows = keys_all[0][:, key_dim:]
    query_rows = queries.reshape(coarse_rows * head_count, key_dim)
    scores = jnp.dot(query_rows, key_rows.T, preferred_element_type=jnp.float32)
    weights = jnp.exp(logit_cap * jnp.tanh(scores / logit_cap))
    totals = jnp.sum(weights, axis=-1, keepdims=True)
    mixed = (
        jnp.dot(weights.astype(jnp.bfloat16), value_rows, preferred_element_type=jnp.float32)
        / totals
    )
    heads_out = mixed.astype(jnp.bfloat16).reshape(coarse_rows, head_count * value_rows.shape[1])
    block_out = (
        widened + jnp.dot(heads_out, output_weight, preferred_element_type=jnp.float32)
    ).astype(jnp.bfloat16)
    return (block_out[None], pair_out[None], grad_flip)


def solution(mesh):
    placed = (
        P("dp", ("seq", "mp"), None),
        P(None, ("seq", "mp"), None),
        P(),
        P(),
        P(),
        P(),
        P(),
        P(),
        P("dp", ("seq", "mp"), None, None),
        P(),
        P("dp", ("seq", "mp"), None, None),
    )
    return jax.shard_map(
        per_device,
        mesh=mesh,
        in_specs=placed,
        out_specs=(P("dp", ("seq", "mp"), None), P("dp", ("seq", "mp"), None, None), P()),
        check_vma=False,
    )
```

profile of v0, /device:TPU:1, one launch (start us, length us, event | category | flops | bytes accessed | tf_op | source)
XLA Modules:
  0.0 959.2 jit_solution(9439417309653292819)
XLA Ops:
  7.2 2.7 copy.24
  12.0 10.3 %collective-permute-start = (bf16[1,2,1408]{2,1,0:T(2,128)(2,1)S(1)}, bf16[1,2,1408]{2,1,0:T(2,128)(2,1)S(1)}, u32[]{:S(2)}, u32[]{:S(2)}) collective-permute-start(bf16[1,2,1408]{2,1,0:T(2,128)(2,1)S(1)} %get-tuple-element.8), channel_id=1, source_target_pairs={{0,1},{1,2},{2,3},{3,4},{4,5},{5,6},{6,7},{7,8},{8,9},{9,10},{10,1... | collective-permute-start | bytes 16904 | tf_op jit(solution)/shard_map/ppermute | solution.py:19
  24.5 6.0 fusion.20
  30.5 426.3 %all-gather.5.cloned.1.call-done = bf16[5,1408,1536]{2,0,1:T(8,128)(2,1)} async-done(((bf16[5,44,1536]{2,0,1:T(8,128)(2,1)}), bf16[5,1408,1536]{2,0,1:T(8,128)(2,1)}) %all-gather.5.cloned.1.call-update) | async-done | bytes 21626896 | tf_op jit(solution)/shard_map/all_gather | solution.py:73
  456.8 92.6 %fusion.83 = (bf16[1,1408,1536]{2,0,1:T(2,128)(2,1)S(1)}, bf16[1,1408,1536]{2,0,1:T(2,128)(2,1)S(1)}, bf16[1,1408,1536]{2,0,1:T(2,128)(2,1)}, bf16[1,1408,1536]{2,0,1:T(2,128)(2,1)}, bf16[1,1408,1536]{2,0,1:T(2,128)(2,1)}) fusion(bf16[5,1408,1536]{2,0,1:T(8,128)(2,1)} %all-gather.5.cloned.1.call-done), kind=kLoop, calls=%fused_computation.101 | loop fusion | bytes 43253760 | tf_op jit(solution)/shard_map/slice | solution.py:37
  549.4 5.0 fusion.7
  554.5 4.9 fusion.9
  562.3 2.3 fusion.13
  564.6 2.9 reshape.58
  567.5 3.0 reduce_max.9
  570.7 2.3 convolution_convert_fusion
  574.6 105.2 %all-gather.1 = bf16[256,128]{1,0:T(8,128)(2,1)S(1)} all-gather(bf16[8,128]{1,0:T(8,128)(2,1)S(1)} %get-tuple-element.11), channel_id=3, replica_groups=mesh['dp'=8,'seq'=16,'mp'=2] {'seq','mp'}, dimensions={0}, use_global_device_ids=true | all-gather | bytes 67584 | tf_op jit(solution)/shard_map/all_gather | solution.py:98
  681.6 4.6 all-to-all-start
  688.3 1.8 reshape.59
  690.1 9.7 %all-to-all-done = bf16[1,8,256,128]{3,1,0,2:T(8,128)(2,1)} async-done(((bf16[1,8,256,128]{3,1,0,2:T(8,128)(2,1)}), bf16[1,8,256,128]{3,1,0,2:T(8,128)(2,1)}, u32[]{:S(2)}, u32[]{:S(2)}) %all-to-all-start) | async-done | bytes 524320 | tf_op jit(solution)/shard_map/all_to_all | solution.py:104
  699.8 2.2 convolution_bitcast_fusion.1
  702.0 2.3 fusion.51
  704.4 6.7 fusion
  711.1 5.9 fusion.63
  717.0 2.0 copy.30
  719.0 2.3 reshape.60
  721.3 4.0 fusion.15
  725.3 225.9 %all-reduce.3.cloned.1.call-done = f32[128,128]{1,0:T(8,128)} async-done(((f32[128,128]{1,0:T(8,128)}), f32[128,128]{1,0:T(8,128)}) %all-reduce.3.cloned.1.call-update) | async-done | bytes 65552 | tf_op jit(solution)/shard_map/psum | solution.py:112
  951.2 1.5 copy.69
  (47 shorter events, 12.8 us)
Async XLA Ops:
  7.2 679.8 %copy-start = (bf16[1536,1024]{1,0:T(8,128)(2,1)S(1)}, bf16[1536,1024]{1,0:T(8,128)(2,1)}, u32[]{:S(2)}) copy-start(bf16[1536,1024]{1,0:T(8,128)(2,1)} %param.14) | copy-start | bytes 9437188
  7.2 449.6 %all-gather.5.cloned.1.call-start = ((), (), s32[]{:S(2)}) async-start(), calls=%async_computation.1 | async-start | bytes 35684352 | tf_op jit(solution)/shard_map/all_gather | solution.py:73
  9.9 694.5 %all-gather.7.cloned.1.call-start = ((), (), s32[]{:S(2)}) async-start(), calls=%async_computation.3 | async-start | bytes 2703360 | tf_op jit(solution)/shard_map/all_gather | solution.py:97
  10.7 11.6 %collective-permute-start.1 = (bf16[1,2,1408]{2,1,0:T(2,128)(2,1)S(1)}, bf16[1,2,1408]{2,1,0:T(2,128)(2,1)S(1)}, u32[]{:S(2)}, u32[]{:S(2)}) collective-permute-start(bf16[1,2,1408]{2,1,0:T(2,128)(2,1)S(1)} %get-tuple-element.9), channel_id=1, source_target_pairs={{1,0},{2,1},{3,2},{4,3},{5,4},{6,5},{7,6},{8,7},{9,8},{10,9},{11,1... | collective-permute-start | bytes 16904 | tf_op jit(solution)/shard_map/ppermute | solution.py:20
  12.0 11.0 %collective-permute-start = (bf16[1,2,1408]{2,1,0:T(2,128)(2,1)S(1)}, bf16[1,2,1408]{2,1,0:T(2,128)(2,1)S(1)}, u32[]{:S(2)}, u32[]{:S(2)}) collective-permute-start(bf16[1,2,1408]{2,1,0:T(2,128)(2,1)S(1)} %get-tuple-element.8), channel_id=1, source_target_pairs={{0,1},{1,2},{2,3},{3,4},{4,5},{5,6},{6,7},{7,8},{8,9},{9,10},{10,1... | collective-permute-start | bytes 16904 | tf_op jit(solution)/shard_map/ppermute | solution.py:19
  456.8 92.6 %copy-start.4 = (bf16[260,1408]{1,0:T(8,128)(2,1)S(1)}, bf16[260,1408]{1,0:T(8,128)(2,1)}, u32[]{:S(2)}) copy-start(bf16[260,1408]{1,0:T(8,128)(2,1)} %fusion.20) | copy-start | bytes 2196484
  549.4 9.9 %slice-start = ((s8[8650752]{0:T(1024)(128)(4,1)}), s8[4194304]{0:T(1024)(128)(4,1)S(1)}, s32[]{:S(2)}) async-start(s8[8650752]{0:T(1024)(128)(4,1)} %bitcast.79), calls=%async_computation.4 | async-start | bytes 8388608
  549.4 9.9 %slice-start.1 = ((s8[8650752]{0:T(1024)(128)(4,1)}), s8[4194304]{0:T(1024)(128)(4,1)S(1)}, s32[]{:S(2)}) async-start(s8[8650752]{0:T(1024)(128)(4,1)} %bitcast.79), calls=%async_computation.5 | async-start | bytes 8388608
  554.4 4.9 slice-start.2
  560.8 1.4 copy-start.1
  564.6 6.1 copy-start.5
  573.0 106.8 %copy-start.2 = (bf16[1,8,256,128]{3,2,1,0:T(8,128)(2,1)S(1)}, bf16[1,8,256,128]{3,2,1,0:T(8,128)(2,1)}, u32[]{:S(2)}) copy-start(bf16[1,8,256,128]{3,2,1,0:T(8,128)(2,1)} %param.19) | copy-start | bytes 1572868
  679.8 0.6 copy-start.3
  681.6 18.2 %all-to-all-start = ((bf16[1,8,256,128]{3,1,0,2:T(8,128)(2,1)}), bf16[1,8,256,128]{3,1,0,2:T(8,128)(2,1)}, u32[]{:S(2)}, u32[]{:S(2)}) async-start(bf16[1,8,256,128]{3,1,0,2:T(8,128)(2,1)} %copy.31), calls=%async_computation | async-start | bytes 1048576 | tf_op jit(solution)/shard_map/all_to_all | solution.py:104
  686.2 264.9 %all-reduce.3.cloned.1.call-start = ((), (), s32[]{:S(2)}) async-start(), calls=%async_computation.2 | async-start | bytes 131072 | tf_op jit(solution)/shard_map/psum | solution.py:112
  704.4 6.7 copy-start.6
Sparse Core Ops, SparseCore 0:
  11.4 445.3 all-gather.4
  573.2 103.0 all-gather.6
  704.5 246.6 all-reduce.2
where the time goes:
time: 960 us; the launch traced here: 959 us
  waiting for transfers between devices  663 us (69%)
  local copies, waits for them, and re-layouts  108 us (11%)
  blocking collectives  105 us (11%)
  matrix products  41.2 us (4%)
  starting transfers between devices  16.3 us (2%)
  between operations  14 us (1%)
  other arithmetic  11.6 us (1%)
    all_gather x1, waiting for transfers between devices, per_device(): lax.all_gather(conv_weight, ('seq', 'mp'), axis=1, tiled=True)  426 us
    psum x1, waiting for transfers between devices, per_device(): grad_flip = lax.psum(grad_term, ('dp', 'seq', 'mp'))  226 us
    all_gather x1, blocking collectives, per_device(): lax.all_gather(pair_k[None], ('seq', 'mp'), axis=1, tiled=True)  105 us
    slice x1, local copies, waits for them, and re-layouts, tap_sum(): filter_rows[lag_index]  92.6 us
  transfers between devices with their start and end apart: 6, of which 4 were waited for; matrix products, arithmetic and copies ran while one was open for 4% of the time, Pallas kernels for 0%

commit v1 on v0

--- a/solution.py
+++ b/solution.py
@@ -95,7 +95,12 @@
     pair_k = pair_feats[:, pair_dim:]
     keys_all, pairk_all = (
         lax.all_gather(keyvals[None], ("seq", "mp"), axis=1, tiled=True),
-        lax.all_gather(pair_k[None], ("seq", "mp"), axis=1, tiled=True),
+        jnp.concatenate(
+            lax.all_to_all(
+                jnp.stack([pair_k[None]] * lax.axis_size(("seq", "mp"))), ("seq", "mp"), 0, 0
+            ),
+            axis=1,
+        ),
     )
     summed = (
         pair_input[0].astype(jnp.float32)

time: 960 us -> 930 us (0.969)
  blocking collectives: 105 us -> 16.5 us
  waiting for transfers between devices: 663 us -> 719 us
    all_gather x1 -> x0, blocking collectives: 105 us -> none  [per_device(): lax.all_gather(pair_k[None], ('seq', 'mp'), axis=1, tiled=True)]
    all_gather x1, waiting for transfers between devices: 0.02 us -> 61.4 us  [per_device(): lax.all_gather(keyvals[None], ('seq', 'mp'), axis=1, tiled=True)]
    all_to_all x0 -> x1, blocking collectives: none -> 16.5 us  [per_device(): lax.all_to_all(jnp.stack([pair_k[None]] * lax.axis_size(('seq', 'mp'))),...]
  transfers between devices with their start and end apart: 6 -> 6, of which waited for: 4 -> 5; matrix products, arithmetic and copies ran while one was open for 4% -> 4% of each run, Pallas kernels for 0% -> 0%
where the time goes in v1:
time: 930 us; the launch traced here: 929 us
  waiting for transfers between devices  719 us (77%)
  local copies, waits for them, and re-layouts  108 us (12%)
  matrix products  41.2 us (4%)
  starting transfers between devices  18.1 us (2%)
  blocking collectives  16.5 us (2%)
  between operations  14 us (2%)
  other arithmetic  11.6 us (1%)
    all_gather x1, waiting for transfers between devices, per_device(): lax.all_gather(conv_weight, ('seq', 'mp'), axis=1, tiled=True)  426 us
    psum x1, waiting for transfers between devices, per_device(): grad_flip = lax.psum(grad_term, ('dp', 'seq', 'mp'))  220 us
    slice x1, local copies, waits for them, and re-layouts, tap_sum(): filter_rows[lag_index]  92.6 us
    all_gather x1, waiting for transfers between devices, per_device(): lax.all_gather(keyvals[None], ('seq', 'mp'), axis=1, tiled=True)  61.4 us
  transfers between devices with their start and end apart: 6, of which 5 were waited for; matrix products, arithmetic and copies ran while one was open for 4% of the time, Pallas kernels for 0%

profile of v1, /device:TPU:1, one launch (start us, length us, event | category | flops | bytes accessed | tf_op | source)
XLA Modules:
  0.0 929.0 jit_solution(17491234446463642762)
XLA Ops:
  7.2 2.7 copy.24
  12.0 10.3 %collective-permute-start = (bf16[1,2,1408]{2,1,0:T(2,128)(2,1)S(1)}, bf16[1,2,1408]{2,1,0:T(2,128)(2,1)S(1)}, u32[]{:S(2)}, u32[]{:S(2)}) collective-permute-start(bf16[1,2,1408]{2,1,0:T(2,128)(2,1)S(1)} %get-tuple-element.8), channel_id=1, source_target_pairs={{0,1},{1,2},{2,3},{3,4},{4,5},{5,6},{6,7},{7,8},{8,9},{9,10},{10,1... | collective-permute-start | bytes 16904 | tf_op jit(solution)/shard_map/ppermute | solution.py:19
  24.5 6.0 fusion.20
  30.5 426.3 %all-gather.4.cloned.1.call-done = bf16[5,1408,1536]{2,0,1:T(8,128)(2,1)} async-done(((bf16[5,44,1536]{2,0,1:T(8,128)(2,1)}), bf16[5,1408,1536]{2,0,1:T(8,128)(2,1)}) %all-gather.4.cloned.1.call-update) | async-done | bytes 21626896 | tf_op jit(solution)/shard_map/all_gather | solution.py:73
  456.8 92.6 %fusion.83 = (bf16[1,1408,1536]{2,0,1:T(2,128)(2,1)S(1)}, bf16[1,1408,1536]{2,0,1:T(2,128)(2,1)S(1)}, bf16[1,1408,1536]{2,0,1:T(2,128)(2,1)}, bf16[1,1408,1536]{2,0,1:T(2,128)(2,1)}, bf16[1,1408,1536]{2,0,1:T(2,128)(2,1)}) fusion(bf16[5,1408,1536]{2,0,1:T(8,128)(2,1)} %all-gather.4.cloned.1.call-done), kind=kLoop, calls=%fused_computation.102 | loop fusion | bytes 43253760 | tf_op jit(solution)/shard_map/slice | solution.py:37
  549.4 5.0 fusion.7
  554.5 4.9 fusion.9
  562.3 2.3 fusion.13
  564.6 2.9 reshape.69
  567.5 3.0 reduce_max.9
  570.7 2.3 convolution_convert_fusion
  574.6 16.5 %all_to_all.20 = bf16[32,1,8,128]{3,2,1,0:T(8,128)(2,1)S(1)} all-to-all(bf16[32,1,8,128]{3,2,1,0:T(8,128)(2,1)S(1)} %stack.3), channel_id=1, replica_groups=mesh['dp'=8,'seq'=16,'mp'=2] {'seq','mp'}, dimensions={0} | all-to-all | bytes 131072 | tf_op jit(solution)/shard_map/all_to_all | solution.py:99
  592.9 6.5 all-to-all-start.1
  601.5 1.8 reshape.70
  603.2 10.9 %all-to-all-done.1 = bf16[1,8,256,128]{3,1,0,2:T(8,128)(2,1)} async-done(((bf16[1,8,256,128]{3,1,0,2:T(8,128)(2,1)}), bf16[1,8,256,128]{3,1,0,2:T(8,128)(2,1)}, u32[]{:S(2)}, u32[]{:S(2)}) %all-to-all-start.1) | async-done | bytes 524320 | tf_op jit(solution)/shard_map/all_to_all | solution.py:109
  614.1 2.2 convolution_bitcast_fusion.1
  616.3 2.3 fusion.51
  618.7 61.4 %all-gather.6.cloned.1.call-done = bf16[4096,320]{0,1:T(8,128)(2,1)} async-done(((bf16[128,320]{0,1:T(8,128)(2,1)}), bf16[4096,320]{0,1:T(8,128)(2,1)}) %all-gather.6.cloned.1.call-update) | async-done | bytes 2621456 | tf_op jit(solution)/shard_map/all_gather | solution.py:97
  680.1 6.6 fusion
  686.7 5.9 fusion.63
  692.7 2.0 copy.30
  694.7 2.3 reshape.71
  696.9 4.0 fusion.15
  700.9 220.0 %all-reduce.3.cloned.1.call-done = f32[128,128]{1,0:T(8,128)} async-done(((f32[128,128]{1,0:T(8,128)}), f32[128,128]{1,0:T(8,128)}) %all-reduce.3.cloned.1.call-update) | async-done | bytes 65552 | tf_op jit(solution)/shard_map/psum | solution.py:117
  (48 shorter events, 14.3 us)
Async XLA Ops:
  7.2 593.0 %copy-start = (bf16[1536,1024]{1,0:T(8,128)(2,1)S(1)}, bf16[1536,1024]{1,0:T(8,128)(2,1)}, u32[]{:S(2)}) copy-start(bf16[1536,1024]{1,0:T(8,128)(2,1)} %param.14) | copy-start | bytes 9437188
  7.2 449.6 %all-gather.4.cloned.1.call-start = ((), (), s32[]{:S(2)}) async-start(), calls=%async_computation.2 | async-start | bytes 35684352 | tf_op jit(solution)/shard_map/all_gather | solution.py:73
  9.9 670.1 %all-gather.6.cloned.1.call-start = ((), (), s32[]{:S(2)}) async-start(), calls=%async_computation.4 | async-start | bytes 2703360 | tf_op jit(solution)/shard_map/all_gather | solution.py:97
  10.7 11.6 %collective-permute-start.1 = (bf16[1,2,1408]{2,1,0:T(2,128)(2,1)S(1)}, bf16[1,2,1408]{2,1,0:T(2,128)(2,1)S(1)}, u32[]{:S(2)}, u32[]{:S(2)}) collective-permute-start(bf16[1,2,1408]{2,1,0:T(2,128)(2,1)S(1)} %get-tuple-element.9), channel_id=1, source_target_pairs={{1,0},{2,1},{3,2},{4,3},{5,4},{6,5},{7,6},{8,7},{9,8},{10,9},{11,1... | collective-permute-start | bytes 16904 | tf_op jit(solution)/shard_map/ppermute | solution.py:20
  12.0 11.0 %collective-permute-start = (bf16[1,2,1408]{2,1,0:T(2,128)(2,1)S(1)}, bf16[1,2,1408]{2,1,0:T(2,128)(2,1)S(1)}, u32[]{:S(2)}, u32[]{:S(2)}) collective-permute-start(bf16[1,2,1408]{2,1,0:T(2,128)(2,1)S(1)} %get-tuple-element.8), channel_id=1, source_target_pairs={{0,1},{1,2},{2,3},{3,4},{4,5},{5,6},{6,7},{7,8},{8,9},{9,10},{10,1... | collective-permute-start | bytes 16904 | tf_op jit(solution)/shard_map/ppermute | solution.py:19
  456.8 92.6 %copy-start.4 = (bf16[260,1408]{1,0:T(8,128)(2,1)S(1)}, bf16[260,1408]{1,0:T(8,128)(2,1)}, u32[]{:S(2)}) copy-start(bf16[260,1408]{1,0:T(8,128)(2,1)} %fusion.20) | copy-start | bytes 2196484
  549.4 9.9 %slice-start = ((s8[8650752]{0:T(1024)(128)(4,1)}), s8[4194304]{0:T(1024)(128)(4,1)S(1)}, s32[]{:S(2)}) async-start(s8[8650752]{0:T(1024)(128)(4,1)} %bitcast.82), calls=%async_computation.5 | async-start | bytes 8388608
  549.4 9.9 %slice-start.1 = ((s8[8650752]{0:T(1024)(128)(4,1)}), s8[4194304]{0:T(1024)(128)(4,1)S(1)}, s32[]{:S(2)}) async-start(s8[8650752]{0:T(1024)(128)(4,1)} %bitcast.82), calls=%async_computation.6 | async-start | bytes 8388608
  554.4 4.9 slice-start.2
  560.8 1.4 copy-start.1
  564.6 6.1 copy-start.5
  573.0 18.1 %copy-start.2 = (bf16[1,8,256,128]{3,2,1,0:T(8,128)(2,1)S(1)}, bf16[1,8,256,128]{3,2,1,0:T(8,128)(2,1)}, u32[]{:S(2)}) copy-start(bf16[1,8,256,128]{3,2,1,0:T(8,128)(2,1)} %param.19) | copy-start | bytes 1572868
  591.1 0.6 copy-start.3
  592.9 21.2 %all-to-all-start.1 = ((bf16[1,8,256,128]{3,1,0,2:T(8,128)(2,1)}), bf16[1,8,256,128]{3,1,0,2:T(8,128)(2,1)}, u32[]{:S(2)}, u32[]{:S(2)}) async-start(bf16[1,8,256,128]{3,1,0,2:T(8,128)(2,1)} %copy.31), calls=%async_computation.1 | async-start | bytes 1048576 | tf_op jit(solution)/shard_map/all_to_all | solution.py:109
  599.4 321.6 %all-reduce.3.cloned.1.call-start = ((), (), s32[]{:S(2)}) async-start(), calls=%async_computation.3 | async-start | bytes 131072 | tf_op jit(solution)/shard_map/psum | solution.py:117
  680.1 6.7 copy-start.6
Sparse Core Ops, SparseCore 0:
  11.4 445.3 all-gather.3
  573.2 106.8 all-gather.5
  686.1 234.7 all-reduce.2
